TPU v7x, 32 devices: a whole 2x2x4 slice. The times are simulated.
32 devices in a mesh: group: 4 (over z), tensor: 4 (over y, core), role: 2 (over x).
Axes of the slice: x: 2, y: 2, z: 4, core: 2. Of those that a mesh axis runs over, the one named last changes fastest.
Arguments:
- queries: bfloat16 [4096, 4096], P(('group', 'role'), 'tensor'), may hold values from -8 to 8
- keys_values: bfloat16 [2, 4096, 1024], P(None, ('group', 'role')), may hold values from -8 to 8
- doc_ids: int32 [4096], P(('group', 'role')), may hold values from 0 to 15, never falling along the last dimension, each value on 1 to 1024 neighbouring positions
Outputs:
- attended: bfloat16 [4096, 4096], P(('group', 'role'), 'tensor')
All inputs are finite; a program needn't handle non-finite values.
Results may differ from a plain program's by a relative error of at most 0.0036.
Values may be sent and summed in bfloat16 or wider, within the bound.
A program may use at most 64 MiB of HBM per device.

v0:
```python
import math
import jax
import jax.numpy as jnp
from jax import lax
from jax.sharding import PartitionSpec as P

HEADS = 32
KV_HEADS = 8
HD = 128


def absorb_keys(running, scores, visible, values, pattern):
    largest, totals, summed = running
    masked = jnp.where(visible, scores, -1e30)
    newest = jnp.maximum(largest, jnp.max(masked, axis=-1))
    factor = jnp.exp(largest - newest)
    weights = jnp.where(visible, jnp.exp(masked - newest[..., None]), 0.0)
    totals = totals * factor + jnp.sum(weights, axis=-1)
    rounded = weights.astype(jnp.bfloat16)
    summed = summed * factor[..., None] + jnp.einsum(
        pattern, rounded, values, preferred_element_type=jnp.float32
    )
    return (newest, totals, summed)


def head_attention(queries, keys_values, doc_ids):
    tok_rows, width_here = queries.shape
    role_index = lax.axis_index("role")
    tensor_index = lax.axis_index("tensor")
    heads_here = width_here // HD
    group_width = HEADS // KV_HEADS
    scaling = 1.0 / math.sqrt(HD)
    kv_count = max(1, heads_here // group_width)
    share = heads_here // kv_count
    first_kv = tensor_index * heads_here // group_width
    own_kv = lax.dynamic_slice_in_dim(keys_values, first_kv * HD, kv_count * HD, 2)[None]
    local_q = queries.reshape(tok_rows, kv_count, share, HD)
    query_pos = role_index * tok_rows + jnp.arange(tok_rows, dtype=jnp.int32)
    row_steps = jnp.arange(tok_rows, dtype=jnp.int32)
    start_state = (
        jnp.full((tok_rows, kv_count, share), -1e30, jnp.float32),
        jnp.zeros((tok_rows, kv_count, share), jnp.float32),
        jnp.zeros((tok_rows, kv_count, share, HD), jnp.float32),
    )
    kv_piece = lax.all_gather(own_kv, "role", axis=0, tiled=True)
    id_piece = lax.all_gather(doc_ids[None], "role", axis=0, tiled=True)

    def one_block(entry, state):

        def take(state_in):
            block = lax.dynamic_index_in_dim(kv_piece, entry, 0, keepdims=False)
            key_ids = lax.dynamic_index_in_dim(id_piece, entry, 0, keepdims=False)
            key_side = block[0].reshape(tok_rows, kv_count, HD)
            value_side = block[1].reshape(tok_rows, kv_count, HD)
            scores = (
                jnp.einsum("qcgd,kcd->qcgk", local_q, key_side, preferred_element_type=jnp.float32)
                * scaling
            )
            key_pos = entry * tok_rows + row_steps
            visible = (key_pos[None, :] <= query_pos[:, None]) & (
                key_ids[None, :] == doc_ids[:, None]
            )
            return absorb_keys(
                state_in, scores, visible[:, None, None, :], value_side, "qcgk,kcd->qcgd"
            )

        def keep(state_in):
            return state_in

        return lax.cond(entry <= role_index, take, keep, state)

    largest, totals, summed = lax.fori_loop(0, kv_piece.shape[0], one_block, start_state)
    return (summed / totals[..., None]).astype(jnp.bfloat16).reshape(tok_rows, width_here)


def per_device(queries, keys_values, doc_ids):
    attended = head_attention(queries, keys_values, doc_ids)
    return attended


def solution(mesh):
    in_specs = (
        P(("group", "role"), "tensor"),
        P(None, ("group", "role"), None),
        P(("group", "role")),
    )
    out_specs = P(("group", "role"), "tensor")
    return jax.shard_map(
        per_device, mesh=mesh, in_specs=in_specs, out_specs=out_specs, check_vma=False
    )
```

profile of v0, /device:TPU:6, one launch (start us, length us, event | category | flops | bytes accessed | tf_op | source)
XLA Modules:
  0.0 64.0 jit_solution(12343102273541048219)
XLA Ops:
  6.5 0.0 copy-start
  6.5 0.0 copy-start.3
  6.5 0.0 all-gather.5.cloned.1.call-start
  6.5 1.6 %copy-done = bf16[2,512,1024]{2,1,0:T(8,128)(2,1)S(1)} copy-done((bf16[2,512,1024]{2,1,0:T(8,128)(2,1)S(1)}, bf16[2,512,1024]{2,1,0:T(8,128)(2,1)}, u32[]{:S(2)}) %copy-start) | copy-done | bytes 2097176
  8.1 0.9 %constant_dynamic-slice_fusion.3 = bf16[2,512,256]{2,1,0:T(8,128)(2,1)} fusion(bf16[2,512,1024]{2,1,0:T(8,128)(2,1)S(1)} %copy-done, s32[]{:T(128)S(6)} %select_n.22), kind=kLoop, calls=%fused_computation.23 | loop fusion | bytes 1048580 | tf_op jit(solution)/shard_map/dynamic_slice | solution.py:36
  9.0 0.0 all-gather.5.cloned.1.call-update
  9.0 2.3 %copy.15 = bf16[512,1024]{0,1:T(8,128)(2,1)} copy(bf16[512,1024]{1,0:T(8,128)(2,1)} %param.7) | data formatting | bytes 2097152 | tf_op args[0]
  11.3 1.6 %copy.17 = bf16[512,2,4,128]{3,0,2,1:T(8,128)(2,1)S(1)} copy(bf16[512,2,4,128]{0,3,2,1:T(8,128)(2,1)} %bitcast.46) | data formatting | bytes 2097152
  12.9 4.5 %all-gather.2 = s32[2,1,512]{2,1,0:T(1,128)S(1)} all-gather(s32[1,1,512]{2,1,0:T(1,128)} %bitcast.54), channel_id=2, replica_groups=mesh['group'=4,'tensor'=4,'role'=2] {'role'}, dimensions={0}, use_global_device_ids=true | all-gather | bytes 6144 | tf_op jit(solution)/shard_map/all_gather | solution.py:46
  17.4 13.3 %all-gather.5.cloned.1.call-done = bf16[4,512,256]{2,1,0:T(8,128)(2,1)} async-done(((bf16[2,512,256]{2,1,0:T(8,128)(2,1)}), bf16[4,512,256]{2,1,0:T(8,128)(2,1)}) %all-gather.5.cloned.1.call-update) | async-done | bytes 1048592 | tf_op jit(solution)/shard_map/all_gather | solution.py:45
  30.7 2.3 %copy.16 = bf16[2,2,512,256]{2,3,1,0:T(8,128)(2,1)} copy(bf16[2,2,512,256]{3,2,1,0:T(8,128)(2,1)} %bitcast.49) | data formatting | bytes 2097152
  33.0 1.6 %broadcast_in_dim.43 = f32[512,2,4,128]{0,3,2,1:T(8,128)} broadcast(f32[]{:T(128)} %constant.57.clone.1), dimensions={} | broadcast | bytes 2097156 | tf_op jit(solution)/shard_map/broadcast_in_dim | solution.py:43
  34.6 0.0 copy-done.3
  34.6 19.3 %while.18 = (s32[]{:T(128)}, f32[512,2,4]{0,2,1:T(4,128)S(1)}, f32[512,2,4]{0,2,1:T(4,128)S(1)}, f32[512,2,4,128]{0,3,2,1:T(8,128)}, s32[]{:T(128)}, /*index=5*/...) while((s32[]{:T(128)}, f32[512,2,4]{0,2,1:T(4,128)S(1)}, ...), condition=%wide.region_5.6_spmd.clone, body=%wide.region_0.5_spmd.clone.sunk | while | flops 1102849024 | bytes 50092432 | solution.py:72
  34.7 9.6 %conditional.3 = ((f32[512,2,4]{0,2,1:T(4,128)S(1)}, f32[512,2,4]{0,2,1:T(4,128)S(1)}, f32[512,2,4,128]{0,3,2,1:T(8,128)})) conditional(s32[]{:T(128)} %convert_element_type.21, (f32[512,2,4]{0,2,1:T(4,128)S(1)}, f32[512,2,4]{0,2,1:T(4,128)S(1)}, f32[512,2,4,128]{0,3,2,1:T(8,128)}) %tuple.49, (s32[]{:T(128)}, s32[512]{0:T(512)S(1)}, s32[]{:T(128)}, ...), branch_computations={%region_1.1_spmd, %region_2.4_spmd} | conditional | flops 1102849024 | bytes 50090148 | solution.py:70
  34.7 0.3 compare_and_fusion
  35.0 1.1 %constant_dynamic-slice_fusion.1 = (bf16[1,1,512,256]{2,3,1,0:T(8,128)(2,1)S(1)}, bf16[1,1,512,256]{2,3,1,0:T(8,128)(2,1)S(1)}) fusion(bf16[2,2,512,256]{2,3,1,0:T(8,128)(2,1)} %get-tuple-element.214, s32[]{:T(128)S(6)} %select_n.16, s32[]{:T(128)S(6)} %add.58), kind=kLoop, calls=%fused_computation.16 | loop fusion | bytes 1048584 | tf_op jit(solution)/shard_map/while/body/eval_jaxpr/cond/branch_1_fun/slice | solution.py:54
  36.1 0.0 copy-start.1
  36.1 2.1 %fusion.4 = (f32[512,2,4]{0,2,1:T(4,128)S(1)}, f32[2,512,512,4]{2,1,3,0:T(8,128)S(1)}) fusion(pred[512,512]{0,1:T(8,128)(4,1)S(1)} %compare_and_fusion, bf16[512,2,128,1]{0,2,3,1:T(8,128)(2,1)S(1)} %bitcast.42, bf16[512,2,4,128]{3,0,2,1:T(8,128)(2,1)S(1)} %get-tuple-element.215), kind=kOutput, calls=%fused_computation.4 | convolution fusion | flops 543158272 | bytes 9977856 | tf_op jit(solution)/shard_map/while/body/eval_jaxpr/cond/branch_1_fun/qcgd,kcd->qcgk/dot_general | solution.py:56
  38.2 2.0 %fusion.6 = f32[512,2,4]{0,2,1:T(4,128)S(1)} fusion(f32[2,512,512,4]{2,1,3,0:T(8,128)S(1)} %get-tuple-element.312, f32[512,2,4]{0,2,1:T(4,128)S(1)} %max.2, pred[512,512]{0,1:T(8,128)(4,1)S(1)} %compare_and_fusion), kind=kLoop, calls=%fused_computation.6 | loop fusion | flops 10481664 | bytes 8683520 | tf_op jit(solution)/shard_map/while/body/eval_jaxpr/cond/branch_1_fun/reduce_sum | solution.py:18
  40.2 0.0 copy-done.1
  40.2 2.7 %bitcast_add_fusion = f32[512,2,4,128]{0,3,2,1:T(8,128)S(1)} fusion(f32[512,2,4,128]{0,3,2,1:T(8,128)S(1)} %copy-done.1, bf16[512,2,128,1]{0,2,3,1:T(8,128)(2,1)S(1)} %bitcast.44, f32[2,512,512,4]{2,1,3,0:T(8,128)S(1)} %get-tuple-element.312, f32[512,2,4]{0,2,1:T(4,128)S(1)} %max.2, pred[512,512]{0,1:T(8,128)(4,1)S(1)} %compare_and_fusion, ...), kind=kOutput, calls=%fused_computation.9 | convolution fusion | flops 548405248 | bytes 13139968 | tf_op jit(solution)/shard_map/while/body/eval_jaxpr/cond/branch_1_fun/qcgk,kcd->qcgd/dot_general | solution.py:20
  43.0 0.0 copy-start.2
  43.0 1.3 %copy-done.2 = f32[512,2,4,128]{0,3,2,1:T(8,128)} copy-done((f32[512,2,4,128]{0,3,2,1:T(8,128)}, f32[512,2,4,128]{0,3,2,1:T(8,128)S(1)}, u32[]{:S(2)}) %copy-start.2) | copy-done | bytes 2097176 | tf_op jit(solution)/shard_map/while/body/eval_jaxpr/cond
  44.3 9.6 %conditional.3 = ((f32[512,2,4]{0,2,1:T(4,128)S(1)}, f32[512,2,4]{0,2,1:T(4,128)S(1)}, f32[512,2,4,128]{0,3,2,1:T(8,128)})) conditional(s32[]{:T(128)} %convert_element_type.21, (f32[512,2,4]{0,2,1:T(4,128)S(1)}, f32[512,2,4]{0,2,1:T(4,128)S(1)}, f32[512,2,4,128]{0,3,2,1:T(8,128)}) %tuple.49, (s32[]{:T(128)}, s32[512]{0:T(512)S(1)}, s32[]{:T(128)}, ...), branch_computations={%region_1.1_spmd, %region_2.4_spmd} | conditional | flops 1102849024 | bytes 50090148 | solution.py:70
  44.3 0.3 compare_and_fusion
  44.6 1.1 %constant_dynamic-slice_fusion.1 = (bf16[1,1,512,256]{2,3,1,0:T(8,128)(2,1)S(1)}, bf16[1,1,512,256]{2,3,1,0:T(8,128)(2,1)S(1)}) fusion(bf16[2,2,512,256]{2,3,1,0:T(8,128)(2,1)} %get-tuple-element.214, s32[]{:T(128)S(6)} %select_n.16, s32[]{:T(128)S(6)} %add.58), kind=kLoop, calls=%fused_computation.16 | loop fusion | bytes 1048584 | tf_op jit(solution)/shard_map/while/body/eval_jaxpr/cond/branch_1_fun/slice | solution.py:54
  45.7 0.0 copy-start.1
  45.7 2.1 %fusion.4 = (f32[512,2,4]{0,2,1:T(4,128)S(1)}, f32[2,512,512,4]{2,1,3,0:T(8,128)S(1)}) fusion(pred[512,512]{0,1:T(8,128)(4,1)S(1)} %compare_and_fusion, bf16[512,2,128,1]{0,2,3,1:T(8,128)(2,1)S(1)} %bitcast.42, bf16[512,2,4,128]{3,0,2,1:T(8,128)(2,1)S(1)} %get-tuple-element.215), kind=kOutput, calls=%fused_computation.4 | convolution fusion | flops 543158272 | bytes 9977856 | tf_op jit(solution)/shard_map/while/body/eval_jaxpr/cond/branch_1_fun/qcgd,kcd->qcgk/dot_general | solution.py:56
  47.8 2.0 %fusion.6 = f32[512,2,4]{0,2,1:T(4,128)S(1)} fusion(f32[2,512,512,4]{2,1,3,0:T(8,128)S(1)} %get-tuple-element.312, f32[512,2,4]{0,2,1:T(4,128)S(1)} %max.2, pred[512,512]{0,1:T(8,128)(4,1)S(1)} %compare_and_fusion), kind=kLoop, calls=%fused_computation.6 | loop fusion | flops 10481664 | bytes 8683520 | tf_op jit(solution)/shard_map/while/body/eval_jaxpr/cond/branch_1_fun/reduce_sum | solution.py:18
  49.9 0.0 copy-done.1
  49.9 2.7 %bitcast_add_fusion = f32[512,2,4,128]{0,3,2,1:T(8,128)S(1)} fusion(f32[512,2,4,128]{0,3,2,1:T(8,128)S(1)} %copy-done.1, bf16[512,2,128,1]{0,2,3,1:T(8,128)(2,1)S(1)} %bitcast.44, f32[2,512,512,4]{2,1,3,0:T(8,128)S(1)} %get-tuple-element.312, f32[512,2,4]{0,2,1:T(4,128)S(1)} %max.2, pred[512,512]{0,1:T(8,128)(4,1)S(1)} %compare_and_fusion, ...), kind=kOutput, calls=%fused_computation.9 | convolution fusion | flops 548405248 | bytes 13139968 | tf_op jit(solution)/shard_map/while/body/eval_jaxpr/cond/branch_1_fun/qcgk,kcd->qcgd/dot_general | solution.py:20
  52.6 0.0 copy-start.2
  52.6 1.3 %copy-done.2 = f32[512,2,4,128]{0,3,2,1:T(8,128)} copy-done((f32[512,2,4,128]{0,3,2,1:T(8,128)}, f32[512,2,4,128]{0,3,2,1:T(8,128)S(1)}, u32[]{:S(2)}) %copy-start.2) | copy-done | bytes 2097176 | tf_op jit(solution)/shard_map/while/body/eval_jaxpr/cond
  53.9 1.9 %divide_convert_fusion = bf16[512,2,4,128]{0,3,2,1:T(8,128)(2,1)S(1)} fusion(f32[512,2,4,128]{0,3,2,1:T(8,128)} %get-tuple-element.235, f32[512,2,4]{0,2,1:T(4,128)S(1)} %get-tuple-element.236), kind=kLoop, calls=%fused_computation.21 | loop fusion | flops 1048576 | bytes 3162112 | tf_op jit(solution)/shard_map/convert_element_type | solution.py:73
  55.8 1.3 %copy.24 = bf16[512,1024]{1,0:T(8,128)(2,1)} copy(bf16[512,1024]{0,1:T(8,128)(2,1)S(1)} %bitcast.45) | data formatting | bytes 2097152 | tf_op jit(solution)/shard_map/reshape | solution.py:73
  (15 shorter events, 0.1 us)
Async XLA Ops:
  6.5 1.6 %copy-start = (bf16[2,512,1024]{2,1,0:T(8,128)(2,1)S(1)}, bf16[2,512,1024]{2,1,0:T(8,128)(2,1)}, u32[]{:S(2)}) copy-start(bf16[2,512,1024]{2,1,0:T(8,128)(2,1)} %param.8) | copy-start | bytes 6291460
  6.5 28.1 %copy-start.3 = (s32[512]{0:T(512)S(1)}, s32[512]{0:T(512)}, u32[]{:S(2)}) copy-start(s32[512]{0:T(512)} %param.9) | copy-start | bytes 6148
  6.5 24.2 %all-gather.5.cloned.1.call-start = ((), (), s32[]{:S(2)}) async-start(), calls=%async_computation | async-start | bytes 1572864 | tf_op jit(solution)/shard_map/all_gather | solution.py:45
  36.1 4.2 %copy-start.1 = (f32[512,2,4,128]{0,3,2,1:T(8,128)S(1)}, f32[512,2,4,128]{0,3,2,1:T(8,128)}, u32[]{:S(2)}) copy-start(f32[512,2,4,128]{0,3,2,1:T(8,128)} %get-tuple-element.217) | copy-start | bytes 6291460 | tf_op jit(solution)/shard_map/while/body/eval_jaxpr/cond
  43.0 1.3 %copy-start.2 = (f32[512,2,4,128]{0,3,2,1:T(8,128)}, f32[512,2,4,128]{0,3,2,1:T(8,128)S(1)}, u32[]{:S(2)}) copy-start(f32[512,2,4,128]{0,3,2,1:T(8,128)S(1)} %bitcast_add_fusion) | copy-start | bytes 6291460 | tf_op jit(solution)/shard_map/while/body/eval_jaxpr/cond
  45.7 4.2 %copy-start.1 = (f32[512,2,4,128]{0,3,2,1:T(8,128)S(1)}, f32[512,2,4,128]{0,3,2,1:T(8,128)}, u32[]{:S(2)}) copy-start(f32[512,2,4,128]{0,3,2,1:T(8,128)} %get-tuple-element.217) | copy-start | bytes 6291460 | tf_op jit(solution)/shard_map/while/body/eval_jaxpr/cond
  52.6 1.3 %copy-start.2 = (f32[512,2,4,128]{0,3,2,1:T(8,128)}, f32[512,2,4,128]{0,3,2,1:T(8,128)S(1)}, u32[]{:S(2)}) copy-start(f32[512,2,4,128]{0,3,2,1:T(8,128)S(1)} %bitcast_add_fusion) | copy-start | bytes 6291460 | tf_op jit(solution)/shard_map/while/body/eval_jaxpr/cond
Sparse Core Ops, SparseCore 0:
  9.2 21.5 all-gather.4
where the time goes:
time: 64.2 us; the launch traced here: 64 us
  local copies, waits for them, and re-layouts  16.4 us (26%)
  between operations  13.4 us (21%)
  waiting for transfers between devices  13.3 us (21%)
  matrix products  9.54 us (15%)
  other arithmetic  6.56 us (10%)
  blocking collectives  4.5 us (7%)
    all_gather x1, waiting for transfers between devices, head_attention(): kv_piece = lax.all_gather(own_kv, 'role', axis=0, tiled=True)  13.3 us
    unnamed x8, local copies, waits for them, and re-layouts  7.75 us
    dot_general x2, matrix products, absorb_keys(): jnp.einsum(pattern, rounded, values, preferred_element_type=jnp.float32)  5.43 us
    all_gather x1, blocking collectives, head_attention(): id_piece = lax.all_gather(doc_ids[None], 'role', axis=0, tiled=True)  4.5 us
    dot_general x2, matrix products, take(): jnp.einsum('qcgd,kcd->qcgk', local_q, key_side, preferred_element_type=jn...  4.1 us
    reduce_sum x2, other arithmetic, absorb_keys(): totals = totals * factor + jnp.sum(weights, axis=-1)  4.09 us
    cond x10, local copies, waits for them, and re-layouts  2.68 us
    slice x2, local copies, waits for them, and re-layouts, take(): value_side = block[1].reshape(tok_rows, kv_count, HD)  2.14 us
  transfers between devices with their start and end apart: 1, of which 1 were waited for; matrix products, arithmetic and copies ran while one was open for 6% of the time, Pallas kernels for 0%

commit v1 on v0

--- a/solution.py
+++ b/solution.py
@@ -1,3 +1,4 @@
+import functools
 import math
 import jax
 import jax.numpy as jnp
@@ -7,6 +8,31 @@
 HEADS = 32
 KV_HEADS = 8
 HD = 128
+
+
+def hubs_post(unit, pos_dim):
+    extra = list(unit.shape[1:])
+    extra[pos_dim] *= unit.shape[0]
+    return jnp.moveaxis(unit, 0, pos_dim).reshape(extra)
+
+
+def keep_up_routes_all(inputs, axis_id):
+    n_dev_all = lax.axis_size(axis_id)
+    y1 = inputs[None]
+    for k in range(n_dev_all.bit_length() - 1):
+        prior = 1 << k
+        base_arr = lax.ppermute(y1, axis_id, [(jj, jj ^ prior) for jj in range(n_dev_all)])
+        r_now = jnp.stack([y1, base_arr], 0)
+        kept_arr = lax.axis_index(axis_id) >> k & 1
+        y1 = jnp.where(kept_arr == 0, r_now, r_now[::-1]).reshape(-1, *inputs.shape)
+    return y1
+
+
+def make_state(buf, vals, on_dim):
+    return hubs_post(keep_up_routes_all(buf, vals), on_dim)
+
+
+state_convert = functools.partial(make_state, vals="role", on_dim=0)
 
 
 def absorb_keys(running, scores, visible, values, pattern):
@@ -42,7 +68,7 @@
         jnp.zeros((tok_rows, kv_count, share), jnp.float32),
         jnp.zeros((tok_rows, kv_count, share, HD), jnp.float32),
     )
-    kv_piece = lax.all_gather(own_kv, "role", axis=0, tiled=True)
+    kv_piece = state_convert(own_kv)
     id_piece = lax.all_gather(doc_ids[None], "role", axis=0, tiled=True)
 
     def one_block(entry, state):

time: 64.2 us -> 43.6 us (0.68)
  between operations: 13.4 us -> 0.03 us
  waiting for transfers between devices: 13.3 us -> 0.01 us
  blocking collectives: 4.5 us -> 9.61 us
  other arithmetic: 6.56 us -> 9.04 us
  local copies, waits for them, and re-layouts: 16.4 us -> 14.3 us
    all_gather x1 -> x0, waiting for transfers between devices: 13.3 us -> none  [head_attention(): kv_piece = lax.all_gather(own_kv, 'role', axis=0, tiled=True)]
    all_gather x1, blocking collectives: 4.5 us -> 9.61 us  [head_attention(): id_piece = lax.all_gather(doc_ids[None], 'role', axis=0, tiled=True)]
    another operation x0 -> x2, other arithmetic: none -> 2.47 us  [the longest x1 1.3 us: keep_up_routes_all(): r_now = jnp.stack([y1, base_arr], 0)]
    unnamed x8 -> x7, local copies, waits for them, and re-layouts: 7.75 us -> 5.48 us
  transfers between devices with their start and end apart: 1 -> 1, of which waited for: 1 -> 0; matrix products, arithmetic and copies ran while one was open for 6% -> 9% of each run, Pallas kernels for 0% -> 0%
where the time goes in v1:
time: 43.6 us; the launch traced here: 43.3 us
  local copies, waits for them, and re-layouts  14.3 us (33%)
  blocking collectives  9.61 us (22%)
  matrix products  9.54 us (22%)
  other arithmetic  9.04 us (21%)
  starting transfers between devices  0.53 us (1%)
    all_gather x1, blocking collectives, head_attention(): id_piece = lax.all_gather(doc_ids[None], 'role', axis=0, tiled=True)  9.61 us
    unnamed x7, local copies, waits for them, and re-layouts  5.48 us
    dot_general x2, matrix products, absorb_keys(): jnp.einsum(pattern, rounded, values, preferred_element_type=jnp.float32)  5.44 us
    dot_general x2, matrix products, take(): jnp.einsum('qcgd,kcd->qcgk', local_q, key_side, preferred_element_type=jn...  4.1 us
    reduce_sum x2, other arithmetic, absorb_keys(): totals = totals * factor + jnp.sum(weights, axis=-1)  4.09 us
    cond x10, local copies, waits for them, and re-layouts  2.7 us
    slice x2, local copies, waits for them, and re-layouts, take(): value_side = block[1].reshape(tok_rows, kv_count, HD)  2.14 us
    convert_element_type x1, other arithmetic, head_attention(): (summed / totals[..., None]).astype(jnp.bfloat16)  1.87 us
  transfers between devices with their start and end apart: 1, of which 0 were waited for; matrix products, arithmetic and copies ran while one was open for 9% of the time, Pallas kernels for 0%

profile of v1, /device:TPU:6, one launch (start us, length us, event | category | flops | bytes accessed | tf_op | source)
XLA Modules:
  0.0 43.3 jit_solution(3106117150057381736)
XLA Ops:
  0.0 0.0 copy-start
  0.0 0.0 copy-start.3
  0.0 1.6 %copy-done = bf16[2,512,1024]{2,1,0:T(8,128)(2,1)S(1)} copy-done((bf16[2,512,1024]{2,1,0:T(8,128)(2,1)S(1)}, bf16[2,512,1024]{2,1,0:T(8,128)(2,1)}, u32[]{:S(2)}) %copy-start) | copy-done | bytes 2097176
  1.6 0.1 constant_dynamic-slice_fusion.3
  1.7 1.0 %copy.17 = bf16[2,512,256]{1,2,0:T(8,128)(2,1)} copy(bf16[2,512,256]{2,1,0:T(8,128)(2,1)S(1)} %constant_dynamic-slice_fusion.3) | data formatting | bytes 1048576 | tf_op jit(solution)/shard_map/dynamic_slice | solution.py:62
  2.7 0.5 %collective-permute-start = (bf16[1,1,2,512,256]{3,4,2,1,0:T(8,128)(2,1)}, bf16[1,1,2,512,256]{3,4,2,1,0:T(8,128)(2,1)}, u32[]{:S(2)}, u32[]{:S(2)}) collective-permute-start(bf16[1,1,2,512,256]{3,4,2,1,0:T(8,128)(2,1)} %bitcast.10), channel_id=1, source_target_pairs={{0,1},{1,0},{2,3},{3,2},{4,5},{5,4},{6,7},{7,6},{8,9},{9,8},{10,11... | collective-permute-start | bytes 1572872 | tf_op jit(solution)/shard_map/ppermute | solution.py:24
  3.2 2.3 %copy.19 = bf16[512,1024]{0,1:T(8,128)(2,1)} copy(bf16[512,1024]{1,0:T(8,128)(2,1)} %param.7) | data formatting | bytes 2097152 | tf_op args[0]
  5.5 1.6 %copy.20 = bf16[512,2,4,128]{3,0,2,1:T(8,128)(2,1)S(1)} copy(bf16[512,2,4,128]{0,3,2,1:T(8,128)(2,1)} %bitcast.50) | data formatting | bytes 2097152
  7.1 9.6 %all-gather.1 = s32[2,1,512]{2,1,0:T(1,128)S(1)} all-gather(s32[1,1,512]{2,1,0:T(1,128)} %bitcast.57), channel_id=2, replica_groups=mesh['group'=4,'tensor'=4,'role'=2] {'role'}, dimensions={0}, use_global_device_ids=true | all-gather | bytes 6144 | tf_op jit(solution)/shard_map/all_gather | solution.py:72
  16.7 0.0 collective-permute-done
  16.7 1.3 %pad_maximum_fusion = bf16[2,1,1,2,512,256]{4,5,3,0,2,1:T(8,128)(2,1)S(1)} fusion(bf16[1,1,1,2,512,256]{4,5,3,0,2,1:T(8,128)(2,1)} %bitcast.11, bf16[1,1,1,2,512,256]{4,5,3,0,2,1:T(8,128)(2,1)} %bitcast.9), kind=kLoop, calls=%fused_computation.24 | loop fusion | flops 524288 | bytes 2097152 | tf_op jit(solution)/shard_map/stack | solution.py:25
  18.0 1.2 %fusion.15 = bf16[2,2,512,256]{2,3,1,0:T(8,128)(2,1)} fusion(bf16[2,1,1,2,512,256]{4,5,3,0,2,1:T(8,128)(2,1)S(1)} %pad_maximum_fusion, pred[]{:T(512)S(6)} %eq.22), kind=kLoop, calls=%fused_computation.23 | loop fusion | flops 524288 | bytes 2097153 | tf_op jit(solution)/shard_map/reshape;reshape | solution.py:16
  19.2 1.6 %broadcast_in_dim.40 = f32[512,2,4,128]{0,3,2,1:T(8,128)} broadcast(f32[]{:T(128)} %constant.58.clone.1), dimensions={} | broadcast | bytes 2097156 | tf_op jit(solution)/shard_map/broadcast_in_dim | solution.py:69
  20.8 0.0 copy-done.3
  20.8 19.3 %while.18 = (s32[]{:T(128)}, f32[512,2,4]{0,2,1:T(4,128)S(1)}, f32[512,2,4]{0,2,1:T(4,128)S(1)}, f32[512,2,4,128]{0,3,2,1:T(8,128)}, s32[]{:T(128)}, /*index=5*/...) while((s32[]{:T(128)}, f32[512,2,4]{0,2,1:T(4,128)S(1)}, ...), condition=%wide.region_5.6_spmd.clone, body=%wide.region_0.5_spmd.clone.sunk | while | flops 1102849024 | bytes 50092432 | solution.py:98
  20.8 9.7 %conditional.3 = ((f32[512,2,4]{0,2,1:T(4,128)S(1)}, f32[512,2,4]{0,2,1:T(4,128)S(1)}, f32[512,2,4,128]{0,3,2,1:T(8,128)})) conditional(s32[]{:T(128)} %convert_element_type.21, (f32[512,2,4]{0,2,1:T(4,128)S(1)}, f32[512,2,4]{0,2,1:T(4,128)S(1)}, f32[512,2,4,128]{0,3,2,1:T(8,128)}) %tuple.49, (s32[]{:T(128)}, s32[512]{0:T(512)S(1)}, s32[]{:T(128)}, ...), branch_computations={%region_1.1_spmd, %region_2.4_spmd} | conditional | flops 1102849024 | bytes 50090148 | solution.py:96
  20.9 0.3 compare_and_fusion
  21.2 1.1 %constant_dynamic-slice_fusion.1 = (bf16[1,1,512,256]{2,3,1,0:T(8,128)(2,1)S(1)}, bf16[1,1,512,256]{2,3,1,0:T(8,128)(2,1)S(1)}) fusion(bf16[2,2,512,256]{2,3,1,0:T(8,128)(2,1)} %get-tuple-element.214, s32[]{:T(128)S(6)} %select_n.22, s32[]{:T(128)S(6)} %add.58), kind=kLoop, calls=%fused_computation.16 | loop fusion | bytes 1048584 | tf_op jit(solution)/shard_map/while/body/eval_jaxpr/cond/branch_1_fun/slice | solution.py:80
  22.3 0.0 copy-start.1
  22.3 2.1 %fusion.4 = (f32[512,2,4]{0,2,1:T(4,128)S(1)}, f32[2,512,512,4]{2,1,3,0:T(8,128)S(1)}) fusion(pred[512,512]{0,1:T(8,128)(4,1)S(1)} %compare_and_fusion, bf16[512,2,128,1]{0,2,3,1:T(8,128)(2,1)S(1)} %bitcast.46, bf16[512,2,4,128]{3,0,2,1:T(8,128)(2,1)S(1)} %get-tuple-element.215), kind=kOutput, calls=%fused_computation.4 | convolution fusion | flops 543158272 | bytes 9977856 | tf_op jit(solution)/shard_map/while/body/eval_jaxpr/cond/branch_1_fun/qcgd,kcd->qcgk/dot_general | solution.py:82
  24.3 2.0 %fusion.6 = f32[512,2,4]{0,2,1:T(4,128)S(1)} fusion(f32[2,512,512,4]{2,1,3,0:T(8,128)S(1)} %get-tuple-element.312, f32[512,2,4]{0,2,1:T(4,128)S(1)} %max.2, pred[512,512]{0,1:T(8,128)(4,1)S(1)} %compare_and_fusion), kind=kLoop, calls=%fused_computation.6 | loop fusion | flops 10481664 | bytes 8683520 | tf_op jit(solution)/shard_map/while/body/eval_jaxpr/cond/branch_1_fun/reduce_sum | solution.py:44
  26.4 0.0 copy-done.1
  26.4 2.7 %bitcast_add_fusion = f32[512,2,4,128]{0,3,2,1:T(8,128)S(1)} fusion(f32[512,2,4,128]{0,3,2,1:T(8,128)S(1)} %copy-done.1, bf16[512,2,128,1]{0,2,3,1:T(8,128)(2,1)S(1)} %bitcast.48, f32[2,512,512,4]{2,1,3,0:T(8,128)S(1)} %get-tuple-element.312, f32[512,2,4]{0,2,1:T(4,128)S(1)} %max.2, pred[512,512]{0,1:T(8,128)(4,1)S(1)} %compare_and_fusion, ...), kind=kOutput, calls=%fused_computation.9 | convolution fusion | flops 548405248 | bytes 13139968 | tf_op jit(solution)/shard_map/while/body/eval_jaxpr/cond/branch_1_fun/qcgk,kcd->qcgd/dot_general | solution.py:46
  29.2 0.0 copy-start.2
  29.2 1.3 %copy-done.2 = f32[512,2,4,128]{0,3,2,1:T(8,128)} copy-done((f32[512,2,4,128]{0,3,2,1:T(8,128)}, f32[512,2,4,128]{0,3,2,1:T(8,128)S(1)}, u32[]{:S(2)}) %copy-start.2) | copy-done | bytes 2097176 | tf_op jit(solution)/shard_map/while/body/eval_jaxpr/cond
  30.5 9.6 %conditional.3 = ((f32[512,2,4]{0,2,1:T(4,128)S(1)}, f32[512,2,4]{0,2,1:T(4,128)S(1)}, f32[512,2,4,128]{0,3,2,1:T(8,128)})) conditional(s32[]{:T(128)} %convert_element_type.21, (f32[512,2,4]{0,2,1:T(4,128)S(1)}, f32[512,2,4]{0,2,1:T(4,128)S(1)}, f32[512,2,4,128]{0,3,2,1:T(8,128)}) %tuple.49, (s32[]{:T(128)}, s32[512]{0:T(512)S(1)}, s32[]{:T(128)}, ...), branch_computations={%region_1.1_spmd, %region_2.4_spmd} | conditional | flops 1102849024 | bytes 50090148 | solution.py:96
  30.5 0.3 compare_and_fusion
  30.8 1.1 %constant_dynamic-slice_fusion.1 = (bf16[1,1,512,256]{2,3,1,0:T(8,128)(2,1)S(1)}, bf16[1,1,512,256]{2,3,1,0:T(8,128)(2,1)S(1)}) fusion(bf16[2,2,512,256]{2,3,1,0:T(8,128)(2,1)} %get-tuple-element.214, s32[]{:T(128)S(6)} %select_n.22, s32[]{:T(128)S(6)} %add.58), kind=kLoop, calls=%fused_computation.16 | loop fusion | bytes 1048584 | tf_op jit(solution)/shard_map/while/body/eval_jaxpr/cond/branch_1_fun/slice | solution.py:80
  31.9 0.0 copy-start.1
  31.9 2.1 %fusion.4 = (f32[512,2,4]{0,2,1:T(4,128)S(1)}, f32[2,512,512,4]{2,1,3,0:T(8,128)S(1)}) fusion(pred[512,512]{0,1:T(8,128)(4,1)S(1)} %compare_and_fusion, bf16[512,2,128,1]{0,2,3,1:T(8,128)(2,1)S(1)} %bitcast.46, bf16[512,2,4,128]{3,0,2,1:T(8,128)(2,1)S(1)} %get-tuple-element.215), kind=kOutput, calls=%fused_computation.4 | convolution fusion | flops 543158272 | bytes 9977856 | tf_op jit(solution)/shard_map/while/body/eval_jaxpr/cond/branch_1_fun/qcgd,kcd->qcgk/dot_general | solution.py:82
  34.0 2.0 %fusion.6 = f32[512,2,4]{0,2,1:T(4,128)S(1)} fusion(f32[2,512,512,4]{2,1,3,0:T(8,128)S(1)} %get-tuple-element.312, f32[512,2,4]{0,2,1:T(4,128)S(1)} %max.2, pred[512,512]{0,1:T(8,128)(4,1)S(1)} %compare_and_fusion), kind=kLoop, calls=%fused_computation.6 | loop fusion | flops 10481664 | bytes 8683520 | tf_op jit(solution)/shard_map/while/body/eval_jaxpr/cond/branch_1_fun/reduce_sum | solution.py:44
  36.1 0.0 copy-done.1
  36.1 2.7 %bitcast_add_fusion = f32[512,2,4,128]{0,3,2,1:T(8,128)S(1)} fusion(f32[512,2,4,128]{0,3,2,1:T(8,128)S(1)} %copy-done.1, bf16[512,2,128,1]{0,2,3,1:T(8,128)(2,1)S(1)} %bitcast.48, f32[2,512,512,4]{2,1,3,0:T(8,128)S(1)} %get-tuple-element.312, f32[512,2,4]{0,2,1:T(4,128)S(1)} %max.2, pred[512,512]{0,1:T(8,128)(4,1)S(1)} %compare_and_fusion, ...), kind=kOutput, calls=%fused_computation.9 | convolution fusion | flops 548405248 | bytes 13139968 | tf_op jit(solution)/shard_map/while/body/eval_jaxpr/cond/branch_1_fun/qcgk,kcd->qcgd/dot_general | solution.py:46
  38.8 0.0 copy-start.2
  38.8 1.3 %copy-done.2 = f32[512,2,4,128]{0,3,2,1:T(8,128)} copy-done((f32[512,2,4,128]{0,3,2,1:T(8,128)}, f32[512,2,4,128]{0,3,2,1:T(8,128)S(1)}, u32[]{:S(2)}) %copy-start.2) | copy-done | bytes 2097176 | tf_op jit(solution)/shard_map/while/body/eval_jaxpr/cond
  40.1 1.9 %divide_convert_fusion = bf16[512,2,4,128]{0,3,2,1:T(8,128)(2,1)S(1)} fusion(f32[512,2,4,128]{0,3,2,1:T(8,128)} %get-tuple-element.235, f32[512,2,4]{0,2,1:T(4,128)S(1)} %get-tuple-element.236), kind=kLoop, calls=%fused_computation.21 | loop fusion | flops 1048576 | bytes 3162112 | tf_op jit(solution)/shard_map/convert_element_type | solution.py:99
  42.0 1.3 %copy.27 = bf16[512,1024]{1,0:T(8,128)(2,1)} copy(bf16[512,1024]{0,1:T(8,128)(2,1)S(1)} %bitcast.49) | data formatting | bytes 2097152 | tf_op jit(solution)/shard_map/reshape | solution.py:99
  (15 shorter events, 0.1 us)
Async XLA Ops:
  0.0 1.6 %copy-start = (bf16[2,512,1024]{2,1,0:T(8,128)(2,1)S(1)}, bf16[2,512,1024]{2,1,0:T(8,128)(2,1)}, u32[]{:S(2)}) copy-start(bf16[2,512,1024]{2,1,0:T(8,128)(2,1)} %param.8) | copy-start | bytes 6291460
  0.0 20.8 %copy-start.3 = (s32[512]{0:T(512)S(1)}, s32[512]{0:T(512)}, u32[]{:S(2)}) copy-start(s32[512]{0:T(512)} %param.9) | copy-start | bytes 6148
  2.7 14.0 %collective-permute-start = (bf16[1,1,2,512,256]{3,4,2,1,0:T(8,128)(2,1)}, bf16[1,1,2,512,256]{3,4,2,1,0:T(8,128)(2,1)}, u32[]{:S(2)}, u32[]{:S(2)}) collective-permute-start(bf16[1,1,2,512,256]{3,4,2,1,0:T(8,128)(2,1)} %bitcast.10), channel_id=1, source_target_pairs={{0,1},{1,0},{2,3},{3,2},{4,5},{5,4},{6,7},{7,6},{8,9},{9,8},{10,11... | collective-permute-start | bytes 1572872 | tf_op jit(solution)/shard_map/ppermute | solution.py:24
  22.3 4.2 %copy-start.1 = (f32[512,2,4,128]{0,3,2,1:T(8,128)S(1)}, f32[512,2,4,128]{0,3,2,1:T(8,128)}, u32[]{:S(2)}) copy-start(f32[512,2,4,128]{0,3,2,1:T(8,128)} %get-tuple-element.217) | copy-start | bytes 6291460 | tf_op jit(solution)/shard_map/while/body/eval_jaxpr/cond
  29.2 1.3 %copy-start.2 = (f32[512,2,4,128]{0,3,2,1:T(8,128)}, f32[512,2,4,128]{0,3,2,1:T(8,128)S(1)}, u32[]{:S(2)}) copy-start(f32[512,2,4,128]{0,3,2,1:T(8,128)S(1)} %bitcast_add_fusion) | copy-start | bytes 6291460 | tf_op jit(solution)/shard_map/while/body/eval_jaxpr/cond
  31.9 4.2 %copy-start.1 = (f32[512,2,4,128]{0,3,2,1:T(8,128)S(1)}, f32[512,2,4,128]{0,3,2,1:T(8,128)}, u32[]{:S(2)}) copy-start(f32[512,2,4,128]{0,3,2,1:T(8,128)} %get-tuple-element.217) | copy-start | bytes 6291460 | tf_op jit(solution)/shard_map/while/body/eval_jaxpr/cond
  38.8 1.3 %copy-start.2 = (f32[512,2,4,128]{0,3,2,1:T(8,128)}, f32[512,2,4,128]{0,3,2,1:T(8,128)S(1)}, u32[]{:S(2)}) copy-start(f32[512,2,4,128]{0,3,2,1:T(8,128)S(1)} %bitcast_add_fusion) | copy-start | bytes 6291460 | tf_op jit(solution)/shard_map/while/body/eval_jaxpr/cond
